TPU v7x, 32 devices: a whole 2x2x4 slice. The times are simulated.
32 devices in a mesh: dp: 8 (over y, x, core), tensor: 4 (over z).
Axes of the slice: x: 2, y: 2, z: 4, core: 2. Of those that a mesh axis runs over, the one named last changes fastest.
Arguments:
- tokens: bfloat16 [4096, 768], P('dp'), may hold values from -6 to 6
- lengths: int32 [8, 16], P('dp'), may hold values from 0 to 512, as said below
- w_query: bfloat16 [768, 768], P(None, 'tensor'), may hold values from -0.21875 to 0.21875
- w_key: bfloat16 [768, 768], P(None, 'tensor'), may hold values from -0.21875 to 0.21875
- w_value: bfloat16 [768, 768], P(None, 'tensor'), may hold values from -0.21875 to 0.21875
- b_query: float32 [768], P('tensor'), may hold values from -3 to 3
- b_value: float32 [768], P('tensor'), may hold values from -3 to 3
- w_out: bfloat16 [768, 768], P('tensor'), may hold values from -0.625 to 0.625
- b_out: float32 [768], replicated, may hold values from -3 to 3
- g_attn: float32 [768], replicated, may hold values from 0.5 to 1.5
- b_attn: float32 [768], replicated, may hold values from -3 to 3
- w_up: bfloat16 [768, 3072], P(None, 'tensor'), may hold values from -0.21875 to 0.21875
- b_up: float32 [3072], P('tensor'), may hold values from -3 to 3
- w_down: bfloat16 [3072, 768], P('tensor'), may hold values from -0.109375 to 0.109375
- b_down: float32 [768], replicated, may hold values from -3 to 3
- g_ffn: float32 [768], replicated, may hold values from 0.5 to 1.5
- b_ffn: float32 [768], replicated, may hold values from -3 to 3
- out_grad: bfloat16 [4096, 768], P('dp'), may hold values from -6 to 6
- pool_grad: float32 [128, 1728], P('dp'), may hold values from -6 to 6
Outputs:
- layer_out: bfloat16 [4096, 768], P('dp')
- pools: float32 [128, 1728], replicated
- d_tokens: float32 [4096, 768], P('dp')
- d_w_query: float32 [768, 768], P(None, 'tensor')
- d_w_key: float32 [768, 768], P(None, 'tensor')
- d_w_value: float32 [768, 768], P(None, 'tensor')
- d_b_query: float32 [768], P('tensor')
- d_b_value: float32 [768], P('tensor')
- d_w_out: float32 [768, 768], P('tensor')
- d_b_out: float32 [768], replicated
- d_g_attn: float32 [768], replicated
- d_b_attn: float32 [768], replicated
- d_w_up: float32 [768, 3072], P(None, 'tensor')
- d_b_up: float32 [3072], P('tensor')
- d_w_down: float32 [3072, 768], P('tensor')
- d_b_down: float32 [768], replicated
- d_g_ffn: float32 [768], replicated
- d_b_ffn: float32 [768], replicated
Inputs may be any that keep to these rules, and one draw needn't show every extreme that they name: In each bucket the nonzero lengths come first and add up to at most 512; the first is nonzero; in every draw some bucket holds one sentence of exactly 512 tokens.
All inputs are finite; a program needn't handle non-finite values.
Results may differ from a plain program's by a relative error of at most 0.013.
Values sent between devices are 32-bit elements; how exact they have to be, the bound alone decides.
No kernel may reach another device: no remote copies, remote signals or barrier semaphores. Data moves between devices by JAX's collectives and lax.ppermute only.
A program may use at most 128 MiB of HBM per device.

v0:
```python
import jax
import jax.numpy as jnp
from jax import lax
from jax.sharding import PartitionSpec as P

HDIM = 64
SENTS = 16
norm_eps = 1e-06
pool_eps = 1e-05
highest = lax.Precision.HIGHEST


def truncations(width):
    return [width, width * 2 // 3, width // 3, width // 6, width // 12]


def segment_ids(sizes, slot_count):
    ends = jnp.cumsum(sizes, dtype=jnp.int32)
    places = jnp.arange(slot_count, dtype=jnp.int32)
    return jnp.sum((places[:, None] >= ends[None, :]).astype(jnp.int32), axis=1)


def norm_stats(rows):
    centre = jnp.mean(rows, axis=-1, keepdims=True)
    shifted = rows - centre
    inverse = lax.rsqrt(jnp.mean(shifted * shifted, axis=-1, keepdims=True) + norm_eps)
    return (shifted * inverse, inverse)


def norm_back(grad_in, normal, inverse):
    centre = jnp.mean(grad_in, axis=-1, keepdims=True)
    along = jnp.mean(grad_in * normal, axis=-1, keepdims=True)
    return inverse * (grad_in - centre - normal * along)


def gelu_exact(upper):
    return jax.nn.gelu(upper, approximate=False)


def attention_scores(query_heads, key_heads, allowed, score_scale):
    scores = (
        jnp.einsum("qhd,khd->hqk", query_heads, key_heads, preferred_element_type=jnp.float32)
        * score_scale
    )
    return jnp.where(allowed[None], scores, -1000000000.0)


def shards(
    tokens,
    lengths,
    w_query,
    w_key,
    w_value,
    b_query,
    b_value,
    w_out,
    b_out,
    g_attn,
    b_attn,
    w_up,
    b_up,
    w_down,
    b_down,
    g_ffn,
    b_ffn,
    out_grad,
    pool_grad,
):
    slot_count = tokens.shape[0]
    model_width = tokens.shape[1]
    local_cols = w_query.shape[1]
    head_count = local_cols // HDIM
    score_scale = HDIM ** (-0.5)
    segment = segment_ids(lengths[0], slot_count)
    allowed = segment[:, None] == segment[None, :]
    inputs = tokens.astype(jnp.float32)
    query_rows = (jnp.dot(tokens, w_query, preferred_element_type=jnp.float32) + b_query).astype(
        jnp.bfloat16
    )
    key_rows = jnp.dot(tokens, w_key, preferred_element_type=jnp.float32).astype(jnp.bfloat16)
    value_rows = (jnp.dot(tokens, w_value, preferred_element_type=jnp.float32) + b_value).astype(
        jnp.bfloat16
    )
    query_heads = query_rows.reshape(slot_count, head_count, HDIM)
    key_heads = key_rows.reshape(slot_count, head_count, HDIM)
    value_heads = value_rows.reshape(slot_count, head_count, HDIM)
    scores = attention_scores(query_heads, key_heads, allowed, score_scale)
    top_score = jnp.max(scores, axis=-1, keepdims=True)
    log_total = top_score + jnp.log(jnp.sum(jnp.exp(scores - top_score), axis=-1, keepdims=True))
    probs_low = jnp.exp(scores - log_total).astype(jnp.bfloat16)
    mixed = jnp.einsum("hqk,khd->qhd", probs_low, value_heads, preferred_element_type=jnp.float32)
    mixed = mixed.reshape(slot_count, local_cols).astype(jnp.bfloat16)
    partial_value = jnp.dot(mixed, w_out, preferred_element_type=jnp.float32)
    attn_total = lax.psum(partial_value, "tensor")
    normal_attn, inverse_attn = norm_stats(inputs + attn_total + b_out)
    normed = normal_attn * g_attn + b_attn
    normed_low = normed.astype(jnp.bfloat16)
    upper = jnp.dot(normed_low, w_up, preferred_element_type=jnp.float32) + b_up
    act_rows = gelu_exact(upper).astype(jnp.bfloat16)
    down_total = lax.psum(jnp.dot(act_rows, w_down, preferred_element_type=jnp.float32), "tensor")
    normal_ffn, inverse_ffn = norm_stats(normed + down_total + b_down)
    final = normal_ffn * g_ffn + b_ffn
    layer_out = final.astype(jnp.bfloat16)
    sentence = jnp.arange(SENTS, dtype=jnp.int32)
    member = (segment[None, :] == sentence[:, None]).astype(jnp.float32)
    denom = jnp.maximum(lengths[0], 1).astype(jnp.float32)[:, None]
    pooled = jnp.dot(member, final, precision=highest, preferred_element_type=jnp.float32) / denom
    pieces = []
    factors = []
    for keep_width in truncations(model_width):
        leading = pooled[:, :keep_width]
        factor = lax.rsqrt(jnp.mean(leading * leading, axis=1, keepdims=True) + pool_eps)
        pieces.append(leading * factor)
        factors.append(factor)
    pools = lax.all_gather(jnp.concatenate(pieces, axis=1), "dp", axis=0, tiled=True)
    d_pooled = jnp.zeros_like(pooled)
    offset = 0
    for keep_width, factor in zip(truncations(model_width), factors):
        leading = pooled[:, :keep_width]
        upstream = pool_grad[:, offset : offset + keep_width]
        inner = jnp.mean(upstream * leading, axis=1, keepdims=True)
        d_pooled = d_pooled.at[:, :keep_width].add(factor * upstream - leading * factor**3 * inner)
        offset = offset + keep_width
    spread_back = jnp.einsum(
        "st,sd->td", member, d_pooled / denom, precision=highest, preferred_element_type=jnp.float32
    )
    d_final = out_grad.astype(jnp.float32) + spread_back
    g_ffn_part = jnp.sum(d_final * normal_ffn, axis=0)
    b_ffn_part = jnp.sum(d_final, axis=0)
    d_resid = norm_back(d_final * g_ffn, normal_ffn, inverse_ffn)
    b_down_part = jnp.sum(d_resid, axis=0)
    resid_low = d_resid.astype(jnp.bfloat16)
    w_down_part = jnp.einsum("tf,td->fd", act_rows, resid_low, preferred_element_type=jnp.float32)
    d_act = jnp.einsum("td,fd->tf", resid_low, w_down, preferred_element_type=jnp.float32)
    d_upper = jax.vjp(gelu_exact, upper)[1](d_act)[0]
    b_up_part = jnp.sum(d_upper, axis=0)
    upper_low = d_upper.astype(jnp.bfloat16)
    w_up_part = jnp.einsum("td,tf->df", normed_low, upper_low, preferred_element_type=jnp.float32)
    normed_term = jnp.einsum("tf,df->td", upper_low, w_up, preferred_element_type=jnp.float32)
    d_normed = d_resid + lax.psum(normed_term, "tensor")
    g_attn_part = jnp.sum(d_normed * normal_attn, axis=0)
    b_attn_part = jnp.sum(d_normed, axis=0)
    d_hidden = norm_back(d_normed * g_attn, normal_attn, inverse_attn)
    b_out_part = jnp.sum(d_hidden, axis=0)
    hidden_low = d_hidden.astype(jnp.bfloat16)
    w_out_part = jnp.einsum("tc,td->cd", mixed, hidden_low, preferred_element_type=jnp.float32)
    d_mixed = jnp.einsum("td,cd->tc", hidden_low, w_out, preferred_element_type=jnp.float32)
    d_mixed = d_mixed.astype(jnp.bfloat16).reshape(slot_count, head_count, HDIM)
    scores_again = attention_scores(query_heads, key_heads, allowed, score_scale)
    probs = jnp.exp(scores_again - log_total)
    probs_again = probs.astype(jnp.bfloat16)
    d_probs = jnp.einsum("qhd,khd->hqk", d_mixed, value_heads, preferred_element_type=jnp.float32)
    row_inner = jnp.sum(probs * d_probs, axis=-1, keepdims=True)
    d_scores = (probs * (d_probs - row_inner) * score_scale).astype(jnp.bfloat16)
    d_query = jnp.einsum(
        "hqk,khd->qhd", d_scores, key_heads, preferred_element_type=jnp.float32
    ).reshape(slot_count, local_cols)
    d_key = jnp.einsum(
        "hqk,qhd->khd", d_scores, query_heads, preferred_element_type=jnp.float32
    ).reshape(slot_count, local_cols)
    d_value = jnp.einsum(
        "hqk,qhd->khd", probs_again, d_mixed, preferred_element_type=jnp.float32
    ).reshape(slot_count, local_cols)
    b_query_part = jnp.sum(d_query, axis=0)
    b_value_part = jnp.sum(d_value, axis=0)
    query_low = d_query.astype(jnp.bfloat16)
    key_low = d_key.astype(jnp.bfloat16)
    value_low = d_value.astype(jnp.bfloat16)
    w_query_part = jnp.einsum("td,tc->dc", tokens, query_low, preferred_element_type=jnp.float32)
    w_key_part = jnp.einsum("td,tc->dc", tokens, key_low, preferred_element_type=jnp.float32)
    w_value_part = jnp.einsum("td,tc->dc", tokens, value_low, preferred_element_type=jnp.float32)
    input_term = jnp.einsum("tc,dc->td", query_low, w_query, preferred_element_type=jnp.float32)
    input_term = input_term + jnp.einsum(
        "tc,dc->td", key_low, w_key, preferred_element_type=jnp.float32
    )
    input_term = input_term + jnp.einsum(
        "tc,dc->td", value_low, w_value, preferred_element_type=jnp.float32
    )
    d_tokens = d_hidden + lax.psum(input_term, "tensor")
    grad_sums = lax.psum(
        (
            w_query_part,
            w_key_part,
            w_value_part,
            b_query_part,
            b_value_part,
            w_out_part,
            b_out_part,
            g_attn_part,
            b_attn_part,
            w_up_part,
            b_up_part,
            w_down_part,
            b_down_part,
            g_ffn_part,
            b_ffn_part,
        ),
        "dp",
    )
    (
        d_w_query,
        d_w_key,
        d_w_value,
        d_b_query,
        d_b_value,
        d_w_out,
        d_b_out,
        d_g_attn,
        d_b_attn,
        d_w_up,
        d_b_up,
        d_w_down,
        d_b_down,
        d_g_ffn,
        d_b_ffn,
    ) = grad_sums
    return (
        layer_out,
        pools,
        d_tokens,
        d_w_query,
        d_w_key,
        d_w_value,
        d_b_query,
        d_b_value,
        d_w_out,
        d_b_out,
        d_g_attn,
        d_b_attn,
        d_w_up,
        d_b_up,
        d_w_down,
        d_b_down,
        d_g_ffn,
        d_b_ffn,
    )


def solution(mesh):
    return jax.shard_map(
        shards,
        mesh=mesh,
        in_specs=(
            P("dp", None),
            P("dp", None),
            P(None, "tensor"),
            P(None, "tensor"),
            P(None, "tensor"),
            P("tensor"),
            P("tensor"),
            P("tensor", None),
            P(),
            P(),
            P(),
            P(None, "tensor"),
            P("tensor"),
            P("tensor", None),
            P(),
            P(),
            P(),
            P("dp", None),
            P("dp", None),
        ),
        out_specs=(
            P("dp", None),
            P(),
            P("dp", None),
            P(None, "tensor"),
            P(None, "tensor"),
            P(None, "tensor"),
            P("tensor"),
            P("tensor"),
            P("tensor", None),
            P(),
            P(),
            P(),
            P(None, "tensor"),
            P("tensor"),
            P("tensor", None),
            P(),
            P(),
            P(),
        ),
        check_vma=False,
    )
```

profile of v0, /device:TPU:0, one launch (start us, length us, event | category | flops | bytes accessed | tf_op | source)
XLA Modules:
  0.0 486.1 jit_solution(11460330406638272772)
XLA Ops:
  7.3 0.9 copy.49
  8.6 1.7 convolution_convert_fusion.2
  10.4 0.4 fusion.26
  10.8 0.8 fusion.4
  11.7 0.7 exponential_reduce_fusion
  12.4 0.4 copy-done.24
  13.3 1.0 convolution_convert_fusion
  14.3 1.6 fusion.70
  16.0 71.8 %all-reduce.8.cloned.1.call-done = f32[512,768]{1,0:T(8,128)} async-done(((f32[512,768]{1,0:T(8,128)}), f32[512,768]{1,0:T(8,128)}) %all-reduce.8.cloned.1.call-update) | async-done | bytes 1572880 | tf_op jit(solution)/shard_map/psum | solution.py:94
  87.7 1.7 fusion.64
  90.2 5.4 %multiply_convert_fusion.1 = (bf16[512,768]{1,0:T(8,128)(2,1)S(1)}, f32[512,768]{1,0:T(8,128)}, f32[512,768]{1,0:T(8,128)}) fusion(f32[768]{0:T(1024)S(1)} %copy-done.59, bf16[768,768]{1,0:T(8,128)(2,1)S(1)} %copy-done, f32[512,768]{1,0:T(8,128)S(1)} %get-tuple-element.189, f32[768]{0:T(1024)S(1)} %copy-done.53, f32[768]{0:T(1024)S(1)} %copy-done.35, ...), kind=kOutput, calls=%fused_computation.24 | convolution fusion | flops 631898112 | bytes 6697984 | tf_op jit(solution)/shard_map/dot_general | solution.py:98
  95.5 0.9 copy-done.16
  96.4 1.9 fusion.71
  98.6 0.6 compare_reduce_fusion.2
  99.2 0.6 compare_reduce_fusion
  99.9 1.2 convert_bitcast_fusion
  101.0 65.6 %all-reduce.10.cloned.1.call-done = f32[512,768]{1,0:T(8,128)} async-done(((f32[512,768]{1,0:T(8,128)}), f32[512,768]{1,0:T(8,128)}) %all-reduce.10.cloned.1.call-update) | async-done | bytes 1572880 | tf_op jit(solution)/shard_map/psum | solution.py:100
  166.7 2.0 fusion.62
  169.0 0.6 copy-done.28
  169.7 1.0 multiply_reduce_fusion.9
  171.4 0.7 constant_dynamic-update-slice_fusion.4
  172.1 0.7 constant_dynamic-update-slice_fusion.3
  172.8 0.7 constant_dynamic-update-slice_fusion.2
  173.5 1.3 add_select_fusion.2
  174.9 0.6 copy-done.29
  175.5 1.4 scatter-add.19
  177.0 3.9 multiply_reduce_fusion.1
  181.0 1.5 fusion.60
  182.5 0.5 copy-done.65
  183.0 0.5 copy-done.66
  183.5 1.8 fusion.69
  185.3 0.9 copy-done.63
  186.2 2.0 fusion.42
  188.4 68.0 %all-reduce.12.cloned.1.call-done = f32[512,768]{1,0:T(8,128)} async-done(((f32[512,768]{1,0:T(8,128)}), f32[512,768]{1,0:T(8,128)}) %all-reduce.12.cloned.1.call-update) | async-done | bytes 1572880 | tf_op jit(solution)/shard_map/psum | solution.py:140
  256.4 3.3 multiply_reduce_fusion.2
  259.8 1.1 fusion.61
  260.9 1.1 copy-done.2
  262.0 0.4 convolution_convert_fusion.1
  262.5 2.3 fusion.72
  264.8 7.5 %fusion.66 = (f32[3,64]{1,0:T(4,128)}, bf16[512,3,64]{0,2,1:T(8,128)(2,1)S(1)}) fusion(bf16[512,3,64]{0,2,1:T(8,128)(2,1)S(1)} %bitcast.68, f32[3,512,512]{1,2,0:T(8,128)} %fusion.72, f32[3,512]{1,0:T(4,128)S(1)} %copy-done.44, f32[3,512,512]{1,2,0:T(8,128)} %copy-done.8, pred[512,512]{0,1:T(8,128)(4,1)S(1)} %copy-done.12), kind=kOutput, calls=%fused_computation.151 | convolution fusion | flops 109512512 | bytes 6953728 | tf_op jit(solution)/shard_map/hqk,khd->qhd/dot_general | solution.py:155
  272.3 6.9 %fusion.27 = bf16[3,64,512]{2,1,0:T(8,128)(2,1)S(1)} fusion(bf16[512,3,64]{0,2,1:T(8,128)(2,1)} %bitcast.78, f32[3,512,512]{1,2,0:T(8,128)} %fusion.72, f32[3,512,512]{1,2,0:T(8,128)} %copy-done.8, f32[3,512]{1,0:T(4,128)S(1)} %copy-done.44, pred[512,512]{0,1:T(8,128)(4,1)S(1)} %copy-done.12), kind=kOutput, calls=%fused_computation.60 | convolution fusion | flops 109414400 | bytes 6952960 | tf_op jit(solution)/shard_map/hqk,qhd->khd/dot_general | solution.py:158
  279.3 3.6 fusion.65
  283.3 0.5 copy-done.13
  284.2 1.6 add_add_fusion
  285.9 3.9 fusion.44
  289.8 2.4 fusion.40
  292.2 1.1 convolution_bitcast_fusion.2
  293.4 1.1 convolution_bitcast_fusion.1
  294.5 1.1 convolution_bitcast_fusion
  295.7 1.1 fusion.37
  296.9 0.8 copy-done.30
  297.7 10.6 %all_gather.3 = f32[128,1728]{1,0:T(8,128)S(1)} all-gather(f32[16,1728]{1,0:T(8,128)S(1)} %copy-done.30), channel_id=1, replica_groups=mesh['dp'=8,'tensor'=4] {'dp'}, dimensions={0}, use_global_device_ids=true | all-gather | bytes 995328 | tf_op jit(solution)/shard_map/all_gather | solution.py:115
  308.3 1.2 copy.54
  309.7 25.0 %all-reduce = (f32[192]{0:T(256)}, f32[192]{0:T(256)}, f32[768]{0:T(1024)}, f32[768]{0:T(1024)}, f32[768]{0:T(1024)}, /*index=5*/f32[768]{0:T(1024)}, f32[768]{0:T(1024)}, f32[768]{0:T(1024)}, f32[768]{0:T(1024)}) all-reduce(f32[192]{0:T(256)S(1)} %reduce_sum.296, ...), channel_id=1, replica_groups=mesh['dp'=8,'tensor'=4] {'dp'}, use_global_device_ids=true, to_apply=%region_35.36 | all-reduce | flops 5760 | bytes 46080 | tf_op jit(solution)/shard_map/psum | solution.py:180
  334.7 19.3 %all-reduce.14.cloned.1.call-done = f32[512,768]{1,0:T(8,128)} async-done(((f32[512,768]{1,0:T(8,128)}), f32[512,768]{1,0:T(8,128)}) %all-reduce.14.cloned.1.call-update) | async-done | bytes 1572880 | tf_op jit(solution)/shard_map/psum | solution.py:179
  354.1 2.7 add.261
  356.8 114.3 %all-reduce.16.cloned.1.call-done = (f32[768,192]{0,1:T(8,128)}, f32[768,192]{0,1:T(8,128)}, f32[768,192]{0,1:T(8,128)}, f32[192,768]{1,0:T(8,128)}, f32[768,768]{1,0:T(8,128)}, /*index=5*/f32[768,768]{1,0:T(8,128)}) async-done(((f32[768,192]{0,1:T(8,128)}, f32[768,192]{0,1:T(8,128)}, f32[768,192]{0,1:T(8,128)}, f32[192,768]{1,0:T(8,128)}, f32[768,768]{1,0:T(8,128)}, /*index=5*/f32[768,768]{1,0:T(8,128)}), ...) | async-done | bytes 7077904 | tf_op jit(solution)/shard_map/psum | solution.py:180
  471.1 2.0 copy.77
  473.2 0.8 copy.78
  474.0 0.8 copy.79
  474.8 0.8 copy.80
  475.6 1.4 copy.81
  477.0 1.1 copy-done.9
  478.1 1.4 copy.82
  (163 shorter events, 4.5 us)
Async XLA Ops:
  7.2 82.6 %copy-start = (bf16[768,768]{1,0:T(8,128)(2,1)S(1)}, bf16[768,768]{1,0:T(8,128)(2,1)}, u32[]{:S(2)}) copy-start(bf16[768,768]{1,0:T(8,128)(2,1)} %param.42) | copy-start | bytes 3538948
  7.2 3.1 copy-start.4
  7.2 3.1 copy-start.26
  7.2 3.1 copy-start.60
  7.2 80.5 %all-reduce.8.cloned.1.call-start = ((), (), s32[]{:S(2)}) async-start(), calls=%async_computation | async-start | bytes 3145728 | tf_op jit(solution)/shard_map/psum | solution.py:94
  8.6 4.6 copy-start.11
  10.4 1.2 copy-start.19
  11.6 1.7 copy-start.8
  11.6 1.2 copy-start.24
  11.6 1.2 copy-start.61
  12.8 1.5 copy-start.43
  13.2 1.0 copy-start.31
  13.3 1.0 copy-start.14
  14.3 1.6 copy-start.17
  14.3 73.4 %copy-start.52 = (f32[768]{0:T(1024)S(1)}, f32[768]{0:T(1024)}, u32[]{:S(2)}) copy-start(f32[768]{0:T(1024)} %param.39) | copy-start | bytes 9220
  15.9 150.8 %all-reduce.10.cloned.1.call-start = ((), (), s32[]{:S(2)}) async-start(), calls=%async_computation.1 | async-start | bytes 3145728 | tf_op jit(solution)/shard_map/psum | solution.py:100
  90.1 6.3 %copy-start.57 = (bf16[768,768]{1,0:T(8,128)(2,1)S(1)}, bf16[768,768]{1,0:T(8,128)(2,1)}, u32[]{:S(2)}) copy-start(bf16[768,768]{1,0:T(8,128)(2,1)} %param.44) | copy-start | bytes 3538948
  98.4 158.1 %all-reduce.12.cloned.1.call-start = ((), (), s32[]{:S(2)}) async-start(), calls=%async_computation.2 | async-start | bytes 3145728 | tf_op jit(solution)/shard_map/psum | solution.py:140
  168.6 2.1 copy-start.5
  168.6 1.0 copy-start.28
  168.7 1.0 copy-start.45
  168.7 1.0 copy-start.47
  168.7 1.0 copy-start.62
  168.7 2.0 copy-start.36
  169.7 5.9 %copy-start.41 = (f32[512]{0:T(512)}, f32[512]{0:T(512)S(1)}, u32[]{:S(2)}) copy-start(f32[512]{0:T(512)S(1)} %add_rsqrt_fusion) | copy-start | bytes 6148
  173.5 2.0 copy-start.34
  176.9 4.0 copy-start.6
  176.9 4.0 copy-start.37
  176.9 4.0 copy-start.42
  176.9 4.0 copy-start.46
  176.9 4.0 copy-start.48
  180.9 1.6 copy-start.58
  180.9 2.0 copy-start.65
  180.9 2.6 copy-start.66
  182.5 2.8 copy-start.7
  188.2 165.9 %all-reduce.14.cloned.1.call-start = ((), (), s32[]{:S(2)}) async-start(), calls=%async_computation.3 | async-start | bytes 3145728 | tf_op jit(solution)/shard_map/psum | solution.py:179
  259.8 2.2 copy-start.15
  260.9 1.1 copy-start.2
  260.9 1.6 copy-start.32
  262.4 2.4 copy-start.12
  262.5 2.3 copy-start.20
  262.5 2.3 copy-start.44
  279.3 3.6 copy-start.27
  282.8 1.0 copy-start.13
  282.9 1.4 copy-start.25
  285.8 4.0 copy-start.54
  285.8 185.3 %all-reduce.16.cloned.1.call-start = ((), (), s32[]{:S(2)}) async-start(), calls=%async_computation.4 | async-start | bytes 14155776 | tf_op jit(solution)/shard_map/psum | solution.py:180
  285.9 3.9 copy-start.64
  293.4 2.3 copy-start.3
  293.4 2.3 copy-start.18
  296.8 12.7 %copy-start.55 = (f32[3,64]{1,0:T(4,128)S(1)}, f32[3,64]{1,0:T(4,128)}, u32[]{:S(2)}) copy-start(f32[3,64]{1,0:T(4,128)} %get-tuple-element.193) | copy-start | bytes 2308
  296.8 12.8 %copy-start.56 = (f32[3,64]{1,0:T(4,128)S(1)}, f32[3,64]{1,0:T(4,128)}, u32[]{:S(2)}) copy-start(f32[3,64]{1,0:T(4,128)} %get-tuple-element.191) | copy-start | bytes 2308
  296.9 12.9 %copy-start.38 = (f32[768]{0:T(1024)S(1)}, f32[768]{0:T(1024)}, u32[]{:S(2)}) copy-start(f32[768]{0:T(1024)} %get-tuple-element.175) | copy-start | bytes 9220
  296.9 12.8 %copy-start.39 = (f32[768]{0:T(1024)S(1)}, f32[768]{0:T(1024)}, u32[]{:S(2)}) copy-start(f32[768]{0:T(1024)} %get-tuple-element.142) | copy-start | bytes 9220
  296.9 12.8 %copy-start.40 = (f32[768]{0:T(1024)S(1)}, f32[768]{0:T(1024)}, u32[]{:S(2)}) copy-start(f32[768]{0:T(1024)} %get-tuple-element.147) | copy-start | bytes 9220
  296.9 12.8 %copy-start.49 = (f32[768]{0:T(1024)S(1)}, f32[768]{0:T(1024)}, u32[]{:S(2)}) copy-start(f32[768]{0:T(1024)} %get-tuple-element.140) | copy-start | bytes 9220
  296.9 12.8 %copy-start.50 = (f32[768]{0:T(1024)S(1)}, f32[768]{0:T(1024)}, u32[]{:S(2)}) copy-start(f32[768]{0:T(1024)} %get-tuple-element.146) | copy-start | bytes 9220
  296.9 12.8 %copy-start.51 = (f32[768]{0:T(1024)S(1)}, f32[768]{0:T(1024)}, u32[]{:S(2)}) copy-start(f32[768]{0:T(1024)} %get-tuple-element.219) | copy-start | bytes 9220
  471.1 2.1 copy-start.23
  471.1 2.9 copy-start.22
  471.1 3.7 copy-start.21
  473.2 2.5 copy-start.10
  475.6 2.5 copy-start.9
  475.6 3.9 copy-start.1
  (8 other events, 6.2 us)
Sparse Core Ops, SparseCore 0:
  16.0 71.6 all-reduce.7
  98.5 68.1 all-reduce.9
  188.3 68.1 all-reduce.11
  285.9 68.0 all-reduce.13
  359.1 111.9 all-reduce.15
where the time goes:
time: 487 us; the launch traced here: 486 us
  waiting for transfers between devices  339 us (70%)
  matrix products  55.8 us (11%)
  blocking collectives  35.6 us (7%)
  other arithmetic  20.7 us (4%)
  local copies, waits for them, and re-layouts  19.7 us (4%)
  between operations  14.5 us (3%)
    psum x1, waiting for transfers between devices, shards(): lax.psum((w_query_part, w_key_part, w_value_part, b_query_part, b_value_p...  114 us
    psum x1, waiting for transfers between devices, shards(): attn_total = lax.psum(partial_value, 'tensor')  71.8 us
    psum x1, waiting for transfers between devices, shards(): d_normed = d_resid + lax.psum(normed_term, 'tensor')  68 us
    psum x1, waiting for transfers between devices, shards(): lax.psum(jnp.dot(act_rows, w_down, preferred_element_type=jnp.float32), '...  65.6 us
    psum x1, blocking collectives, shards(): lax.psum((w_query_part, w_key_part, w_value_part, b_query_part, b_value_p...  25 us
    psum x1, waiting for transfers between devices, shards(): d_tokens = d_hidden + lax.psum(input_term, 'tensor')  19.3 us
    unnamed x141, local copies, waits for them, and re-layouts  17.3 us
    all_gather x1, blocking collectives, shards(): lax.all_gather(jnp.concatenate(pieces, axis=1), 'dp', axis=0, tiled=True)  10.6 us
  transfers between devices with their start and end apart: 5, of which 5 were waited for; matrix products, arithmetic and copies ran while one was open for 4% of the time, Pallas kernels for 0%

commit v1 on v0

--- a/solution.py
+++ b/solution.py
@@ -97,7 +97,10 @@
     normed_low = normed.astype(jnp.bfloat16)
     upper = jnp.dot(normed_low, w_up, preferred_element_type=jnp.float32) + b_up
     act_rows = gelu_exact(upper).astype(jnp.bfloat16)
-    down_total = lax.psum(jnp.dot(act_rows, w_down, preferred_element_type=jnp.float32), "tensor")
+    down_total = jnp.sum(
+        lax.all_gather(jnp.dot(act_rows, w_down, preferred_element_type=jnp.float32), "tensor"),
+        axis=0,
+    )
     normal_ffn, inverse_ffn = norm_stats(normed + down_total + b_down)
     final = normal_ffn * g_ffn + b_ffn
     layer_out = final.astype(jnp.bfloat16)

time: 487 us -> 534 us (1.097)
  waiting for transfers between devices: 339 us -> 385 us
    all_gather x0 -> x1, waiting for transfers between devices: none -> 112 us  [shards(): lax.all_gather(jnp.dot(act_rows, w_down, preferred_element_type=jnp.float...]
    psum x1 -> x0, waiting for transfers between devices: 65.6 us -> none  [shards(): lax.psum(jnp.dot(act_rows, w_down, preferred_element_type=jnp.float32), '...]
    unnamed x141 -> x133, local copies, waits for them, and re-layouts: 17.3 us -> 18.4 us
  transfers between devices with their start and end apart: 5 -> 5, of which waited for: 5 -> 5; matrix products, arithmetic and copies ran while one was open for 4% -> 3% of each run, Pallas kernels for 0% -> 0%
where the time goes in v1:
time: 534 us; the launch traced here: 533 us
  waiting for transfers between devices  385 us (72%)
  matrix products  52.8 us (10%)
  blocking collectives  35.6 us (7%)
  other arithmetic  24 us (4%)
  local copies, waits for them, and re-layouts  20.9 us (4%)
  between operations  14.5 us (3%)
    psum x1, waiting for transfers between devices, shards(): lax.psum((w_query_part, w_key_part, w_value_part, b_query_part, b_value_p...  114 us
    all_gather x1, waiting for transfers between devices, shards(): lax.all_gather(jnp.dot(act_rows, w_down, preferred_element_type=jnp.float...  112 us
    psum x1, waiting for transfers between devices, shards(): attn_total = lax.psum(partial_value, 'tensor')  71.8 us
    psum x1, waiting for transfers between devices, shards(): d_normed = d_resid + lax.psum(normed_term, 'tensor')  67 us
    psum x1, blocking collectives, shards(): lax.psum((w_query_part, w_key_part, w_value_part, b_query_part, b_value_p...  25 us
    psum x1, waiting for transfers between devices, shards(): d_tokens = d_hidden + lax.psum(input_term, 'tensor')  19.4 us
    unnamed x133, local copies, waits for them, and re-layouts  18.4 us
  transfers between devices with their start and end apart: 5, of which 5 were waited for; matrix products, arithmetic and copies ran while one was open for 3% of the time, Pallas kernels for 0%

profile of v1, /device:TPU:0, one launch (start us, length us, event | category | flops | bytes accessed | tf_op | source)
XLA Modules:
  0.0 532.9 jit_solution(14862133394301140429)
XLA Ops:
  7.3 0.9 copy.49
  8.6 1.7 convolution_convert_fusion.2
  10.8 0.8 fusion.4
  11.7 0.7 exponential_reduce_fusion
  12.4 0.4 copy-done.25
  13.3 1.0 convolution_convert_fusion
  14.3 0.7 copy-done.18
  15.0 1.6 fusion.70
  16.6 71.8 %all-reduce.7.cloned.1.call-done = f32[512,768]{1,0:T(8,128)} async-done(((f32[512,768]{1,0:T(8,128)}), f32[512,768]{1,0:T(8,128)}) %all-reduce.7.cloned.1.call-update) | async-done | bytes 1572880 | tf_op jit(solution)/shard_map/psum | solution.py:94
  88.4 1.7 fusion.64
  90.8 5.4 %multiply_convert_fusion.1 = (bf16[512,768]{1,0:T(8,128)(2,1)S(1)}, f32[512,768]{1,0:T(8,128)}, f32[512,768]{1,0:T(8,128)}) fusion(f32[768]{0:T(1024)S(1)} %copy-done.55, bf16[768,768]{1,0:T(8,128)(2,1)S(1)} %copy-done, f32[512,768]{1,0:T(8,128)S(1)} %get-tuple-element.189, f32[768]{0:T(1024)S(1)} %copy-done.51, f32[768]{0:T(1024)S(1)} %copy-done.36, ...), kind=kOutput, calls=%fused_computation.24 | convolution fusion | flops 631898112 | bytes 6697984 | tf_op jit(solution)/shard_map/dot_general | solution.py:98
  96.2 0.9 copy-done.17
  97.1 1.9 fusion.71
  99.3 0.6 compare_reduce_fusion.2
  99.9 0.6 compare_reduce_fusion
  100.6 1.2 convert_bitcast_fusion
  101.7 112.0 %all-gather.3.cloned.1.call-done = f32[2048,768]{1,0:T(8,128)} async-done(((f32[512,768]{1,0:T(8,128)}), f32[2048,768]{1,0:T(8,128)}) %all-gather.3.cloned.1.call-update) | async-done | bytes 6291472 | tf_op jit(solution)/shard_map/all_gather | solution.py:101
  213.7 4.5 reduce_sum.287
  218.2 2.0 fusion.62
  220.6 0.6 copy-done.29
  221.2 1.0 multiply_reduce_fusion.9
  222.9 0.7 constant_dynamic-update-slice_fusion.4
  223.6 0.7 constant_dynamic-update-slice_fusion.3
  224.4 0.7 constant_dynamic-update-slice_fusion.2
  225.1 1.3 add_select_fusion.2
  226.4 0.6 copy-done.30
  227.1 1.4 scatter-add.19
  228.5 3.9 multiply_reduce_fusion.1
  232.5 1.5 fusion.60
  234.0 0.5 copy-done.61
  234.5 0.5 copy-done.62
  235.0 1.8 fusion.69
  236.8 0.9 copy-done.59
  237.7 2.0 fusion.42
  240.0 67.0 %all-reduce.9.cloned.1.call-done = f32[512,768]{1,0:T(8,128)} async-done(((f32[512,768]{1,0:T(8,128)}), f32[512,768]{1,0:T(8,128)}) %all-reduce.9.cloned.1.call-update) | async-done | bytes 1572880 | tf_op jit(solution)/shard_map/psum | solution.py:143
  307.0 2.7 multiply_reduce_fusion.2
  309.8 0.5 fusion.61
  311.1 1.2 copy-done.9
  312.3 1.1 fusion.65
  313.4 2.3 fusion.72
  315.7 7.0 %fusion.66 = (f32[3,64]{1,0:T(4,128)S(1)}, bf16[512,3,64]{0,2,1:T(8,128)(2,1)S(1)}) fusion(bf16[512,3,64]{0,2,1:T(8,128)(2,1)S(1)} %bitcast.70, f32[3,512,512]{1,2,0:T(8,128)} %fusion.72, f32[3,512]{1,0:T(4,128)S(1)} %copy-done.42, f32[3,512,512]{1,2,0:T(8,128)} %copy-done.8, pred[512,512]{0,1:T(8,128)(4,1)S(1)} %copy-done.13), kind=kOutput, calls=%fused_computation.151 | convolution fusion | flops 109512512 | bytes 6953728 | tf_op jit(solution)/shard_map/hqk,khd->qhd/dot_general | solution.py:158
  322.7 6.9 %fusion.27 = bf16[3,64,512]{2,1,0:T(8,128)(2,1)S(1)} fusion(bf16[512,3,64]{0,2,1:T(8,128)(2,1)} %bitcast.80, f32[3,512,512]{1,2,0:T(8,128)} %fusion.72, f32[3,512,512]{1,2,0:T(8,128)} %copy-done.8, f32[3,512]{1,0:T(4,128)S(1)} %copy-done.42, pred[512,512]{0,1:T(8,128)(4,1)S(1)} %copy-done.13), kind=kOutput, calls=%fused_computation.60 | convolution fusion | flops 109414400 | bytes 6952960 | tf_op jit(solution)/shard_map/hqk,qhd->khd/dot_general | solution.py:161
  330.1 0.5 copy-done.28
  331.0 1.6 add_add_fusion
  332.7 3.9 fusion.44
  336.6 2.4 fusion.40
  339.0 1.1 convolution_bitcast_fusion
  340.2 1.1 convolution_bitcast_fusion.1
  341.3 1.1 convolution_bitcast_fusion.2
  342.5 1.1 fusion.37
  343.7 0.8 copy-done.31
  344.5 10.6 %all_gather.11 = f32[128,1728]{1,0:T(8,128)S(1)} all-gather(f32[16,1728]{1,0:T(8,128)S(1)} %copy-done.31), channel_id=1, replica_groups=mesh['dp'=8,'tensor'=4] {'dp'}, dimensions={0}, use_global_device_ids=true | all-gather | bytes 995328 | tf_op jit(solution)/shard_map/all_gather | solution.py:118
  355.1 1.2 copy.54
  356.5 25.0 %all-reduce = (f32[192]{0:T(256)}, f32[192]{0:T(256)}, f32[768]{0:T(1024)}, f32[768]{0:T(1024)}, f32[768]{0:T(1024)}, /*index=5*/f32[768]{0:T(1024)}, f32[768]{0:T(1024)}, f32[768]{0:T(1024)}, f32[768]{0:T(1024)}) all-reduce(f32[192]{0:T(256)S(1)} %reduce_sum.306, ...), channel_id=1, replica_groups=mesh['dp'=8,'tensor'=4] {'dp'}, use_global_device_ids=true, to_apply=%region_35.36 | all-reduce | flops 5760 | bytes 46080 | tf_op jit(solution)/shard_map/psum | solution.py:183
  381.5 19.4 %all-reduce.11.cloned.1.call-done = f32[512,768]{1,0:T(8,128)} async-done(((f32[512,768]{1,0:T(8,128)}), f32[512,768]{1,0:T(8,128)}) %all-reduce.11.cloned.1.call-update) | async-done | bytes 1572880 | tf_op jit(solution)/shard_map/psum | solution.py:182
  400.9 2.7 add.259
  403.6 114.3 %all-reduce.13.cloned.1.call-done = (f32[768,192]{0,1:T(8,128)}, f32[768,192]{0,1:T(8,128)}, f32[768,192]{0,1:T(8,128)}, f32[192,768]{1,0:T(8,128)}, f32[768,768]{1,0:T(8,128)}, /*index=5*/f32[768,768]{1,0:T(8,128)}) async-done(((f32[768,192]{0,1:T(8,128)}, f32[768,192]{0,1:T(8,128)}, f32[768,192]{0,1:T(8,128)}, f32[192,768]{1,0:T(8,128)}, f32[768,768]{1,0:T(8,128)}, /*index=5*/f32[768,768]{1,0:T(8,128)}), ...) | async-done | bytes 7077904 | tf_op jit(solution)/shard_map/psum | solution.py:183
  517.9 2.0 copy.76
  520.0 0.8 copy.77
  520.8 0.8 copy.78
  521.6 0.8 copy.79
  522.5 1.4 copy.80
  523.9 1.1 copy-done.10
  525.0 1.4 copy.81
  (156 shorter events, 5.7 us)
Async XLA Ops:
  7.2 83.3 %copy-start = (bf16[768,768]{1,0:T(8,128)(2,1)S(1)}, bf16[768,768]{1,0:T(8,128)(2,1)}, u32[]{:S(2)}) copy-start(bf16[768,768]{1,0:T(8,128)(2,1)} %param.42) | copy-start | bytes 3538948
  7.2 3.1 copy-start.4
  7.2 3.1 copy-start.27
  7.2 3.1 copy-start.56
  7.2 81.2 %all-reduce.7.cloned.1.call-start = ((), (), s32[]{:S(2)}) async-start(), calls=%async_computation | async-start | bytes 3145728 | tf_op jit(solution)/shard_map/psum | solution.py:94
  8.6 4.6 copy-start.12
  10.4 1.2 copy-start.20
  10.8 0.8 copy-start.34
  11.6 1.7 copy-start.8
  11.6 1.2 copy-start.25
  11.6 1.2 copy-start.57
  12.8 1.5 copy-start.41
  13.2 1.1 copy-start.32
  13.3 1.7 copy-start.15
  15.0 73.4 %copy-start.50 = (f32[768]{0:T(1024)S(1)}, f32[768]{0:T(1024)}, u32[]{:S(2)}) copy-start(f32[768]{0:T(1024)} %param.39) | copy-start | bytes 9220
  16.6 197.1 %all-gather.3.cloned.1.call-start = ((), (), s32[]{:S(2)}) async-start(), calls=%async_computation.3 | async-start | bytes 7864320 | tf_op jit(solution)/shard_map/all_gather | solution.py:101
  90.1 0.7 copy-start.55
  90.8 6.3 %copy-start.53 = (bf16[768,768]{1,0:T(8,128)(2,1)S(1)}, bf16[768,768]{1,0:T(8,128)(2,1)}, u32[]{:S(2)}) copy-start(bf16[768,768]{1,0:T(8,128)(2,1)} %param.44) | copy-start | bytes 3538948
  96.2 0.9 copy-start.17
  99.0 208.0 %all-reduce.9.cloned.1.call-start = ((), (), s32[]{:S(2)}) async-start(), calls=%async_computation.1 | async-start | bytes 3145728 | tf_op jit(solution)/shard_map/psum | solution.py:143
  220.2 2.1 copy-start.5
  220.2 1.0 copy-start.29
  220.2 1.0 copy-start.43
  220.2 1.0 copy-start.45
  220.2 1.0 copy-start.58
  220.2 2.0 copy-start.37
  221.2 5.9 %copy-start.39 = (f32[512]{0:T(512)}, f32[512]{0:T(512)S(1)}, u32[]{:S(2)}) copy-start(f32[512]{0:T(512)S(1)} %add_rsqrt_fusion) | copy-start | bytes 6148
  225.1 2.0 copy-start.35
  228.5 4.0 copy-start.6
  228.5 4.0 copy-start.38
  228.5 4.0 copy-start.40
  228.5 4.0 copy-start.44
  228.5 4.0 copy-start.46
  232.5 1.6 copy-start.54
  232.5 2.0 copy-start.61
  232.5 2.6 copy-start.62
  234.0 2.8 copy-start.7
  236.8 0.9 copy-start.59
  239.7 161.2 %all-reduce.11.cloned.1.call-start = ((), (), s32[]{:S(2)}) async-start(), calls=%async_computation.2 | async-start | bytes 3145728 | tf_op jit(solution)/shard_map/psum | solution.py:182
  309.8 1.0 copy-start.16
  309.8 2.6 copy-start.9
  310.3 3.1 copy-start.2
  310.3 2.0 copy-start.13
  310.3 2.0 copy-start.42
  312.3 1.1 copy-start.33
  313.4 2.3 copy-start.21
  322.7 7.0 %copy-start.14 = (bf16[768,192]{0,1:T(8,128)(2,1)S(1)}, bf16[768,192]{0,1:T(8,128)(2,1)}, u32[]{:S(2)}) copy-start(bf16[768,192]{0,1:T(8,128)(2,1)} %param.34) | copy-start | bytes 884740
  329.6 1.0 copy-start.28
  329.7 1.4 copy-start.26
  332.6 4.0 copy-start.52
  332.6 185.3 %all-reduce.13.cloned.1.call-start = ((), (), s32[]{:S(2)}) async-start(), calls=%async_computation.4 | async-start | bytes 14155776 | tf_op jit(solution)/shard_map/psum | solution.py:183
  332.7 3.9 copy-start.60
  340.2 2.3 copy-start.3
  340.2 2.3 copy-start.19
  343.6 0.9 copy-start.31
  343.6 12.9 %copy-start.47 = (f32[768]{0:T(1024)S(1)}, f32[768]{0:T(1024)}, u32[]{:S(2)}) copy-start(f32[768]{0:T(1024)} %get-tuple-element.140) | copy-start | bytes 9220
  343.6 12.9 %copy-start.48 = (f32[768]{0:T(1024)S(1)}, f32[768]{0:T(1024)}, u32[]{:S(2)}) copy-start(f32[768]{0:T(1024)} %get-tuple-element.146) | copy-start | bytes 9220
  343.7 12.9 %copy-start.49 = (f32[768]{0:T(1024)S(1)}, f32[768]{0:T(1024)}, u32[]{:S(2)}) copy-start(f32[768]{0:T(1024)} %get-tuple-element.219) | copy-start | bytes 9220
  517.9 2.1 copy-start.24
  517.9 2.9 copy-start.23
  517.9 3.7 copy-start.22
  520.0 2.5 copy-start.11
  522.4 2.5 copy-start.10
  522.5 3.9 copy-start.1
  (4 other events, 2.7 us)
Sparse Core Ops, SparseCore 0:
  16.7 71.6 all-reduce.6
  99.2 114.4 all-gather.2
  239.8 67.1 all-reduce.8
  332.7 68.1 all-reduce.10
  405.9 111.9 all-reduce.12
